TPU v7x, 512 devices: a whole 4x4x16 slice. The times are simulated.
512 devices in a mesh: rows: 128 (over z, y, core), sub: 4 (over x).
Axes of the slice: x: 4, y: 4, z: 16, core: 2. Of those that a mesh axis runs over, the one named last changes fastest.
Arguments:
- factor_a: float32 [131072, 256], P(('rows', 'sub')), may hold values from -6 to 6
- factor_b: float32 [131072, 256], P(('rows', 'sub')), may hold values from -0.0009765625 to 0.0009765625
- value_diffs: float32 [131072, 32], P(('rows', 'sub')), may hold values from -6 to 6
- residual_diffs: float32 [131072, 32], P(('rows', 'sub')), may hold values from -6 to 6
- residual: float32 [131072], P(('rows', 'sub')), may hold values from -6 to 6
Outputs:
- update: float32 [131072], P(('rows', 'sub'))
- new_a: float32 [131072, 256], P(('rows', 'sub'))
- new_b: float32 [131072, 256], P(('rows', 'sub'))
All inputs are finite; a program needn't handle non-finite values.
Results may differ from a plain program's by a relative error of at most 0.0003.
Values sent between devices are 32-bit elements; how exact they have to be, the bound alone decides.
A program may use at most 64 MiB of HBM per device.

v0:
```python
import jax
import jax.numpy as jnp
from jax import lax
from jax.sharding import PartitionSpec as P


def matmul(left, right):
    return jnp.dot(left, right, precision=lax.Precision.HIGHEST, preferred_element_type=jnp.float32)


def small_inverse(lower):
    extent = lower.shape[0]
    diag_inv = 1.0 / jnp.diagonal(lower)
    strict = jnp.tril(lower, -1) * diag_inv[:, None]
    ident = jnp.eye(extent, dtype=lower.dtype)
    result = ident - strict
    power = strict
    for level in range(3):
        power = matmul(power, power)
        result = matmul(result, ident + power)
    return result * diag_inv[None, :]


def lower_inverse(lower):
    extent = lower.shape[0]
    if extent <= 8:
        return small_inverse(lower)
    half = extent // 2
    upper_inv = lower_inverse(lower[:half, :half])
    tail_inv = lower_inverse(lower[half:, half:])
    corner = -matmul(tail_inv, matmul(lower[half:, :half], upper_inv))
    zeros = jnp.zeros((half, extent - half), lower.dtype)
    return jnp.concatenate(
        [jnp.concatenate([upper_inv, zeros], axis=1), jnp.concatenate([corner, tail_inv], axis=1)],
        axis=0,
    )


def tri_solve(matrix, rhs, lower):
    if lower:
        return matmul(lower_inverse(matrix), rhs)
    return matmul(lower_inverse(matrix.T).T, rhs)


def inverse_gram(gram_v):
    low_v = jnp.linalg.cholesky(gram_v)
    low_inv = lower_inverse(low_v)
    return matmul(low_inv.T, low_inv)


def truncate(gram_a, gram_b, width):
    low_a = jnp.linalg.cholesky(gram_a)
    low_b = jnp.linalg.cholesky(gram_b)
    core = matmul(low_a.T, low_b)
    start = matmul(core.T, core[:, :width])
    low_y = jnp.linalg.cholesky(matmul(start.T, start))
    basis = tri_solve(low_y, start.T, True).T
    return (matmul(low_b, basis), tri_solve(low_b.T, basis, False))


def on_device(factor_a, factor_b, value_diffs, residual_diffs, residual):
    width = factor_a.shape[1]
    gram_v = matmul(residual_diffs.T, residual_diffs)
    proj = matmul(factor_b.T, residual_diffs)
    proj_r = matmul(factor_b.T, residual)
    gram_r = matmul(residual_diffs.T, residual)
    sent_v = gram_v
    sent_v, proj, proj_r, gram_r = lax.psum((sent_v, proj, proj_r, gram_r), ("rows", "sub"))
    gram_v = sent_v
    inv_v = inverse_gram(gram_v)
    fresh = value_diffs - matmul(factor_a, proj)
    scaled_v = matmul(residual_diffs, inv_v)
    wide_a = jnp.concatenate([factor_a, fresh], axis=1)
    wide_b = jnp.concatenate([factor_b, scaled_v], axis=1)
    gram_a = matmul(wide_a.T, wide_a)
    gram_b = matmul(wide_b.T, wide_b)
    sent_a = gram_a
    sent_b = gram_b
    sent_a, sent_b = lax.psum((sent_a, sent_b), ("rows", "sub"))
    gram_a = sent_a
    gram_b = sent_b
    coeffs = -matmul(inv_v, gram_r)
    update = -matmul(factor_a, proj_r) + matmul(fresh, coeffs)
    left_map, right_map = truncate(gram_a, gram_b, width)
    return (update, matmul(wide_a, left_map), matmul(wide_b, right_map))


def solution(mesh):
    placed = (
        P(("rows", "sub"), None),
        P(("rows", "sub"), None),
        P(("rows", "sub"), None),
        P(("rows", "sub"), None),
        P(("rows", "sub")),
    )
    return jax.shard_map(
        on_device,
        mesh=mesh,
        in_specs=placed,
        out_specs=(P(("rows", "sub")), P(("rows", "sub"), None), P(("rows", "sub"), None)),
        check_vma=False,
    )
```

profile of v0, /device:TPU:1, one launch (start us, length us, event | category | flops | bytes accessed | tf_op | source)
XLA Modules:
  0.0 957.2 jit_solution(16427618068768078991)
XLA Ops:
  8.1 1.5 fusion.2054
  10.7 111.9 %all-reduce.99 = (f32[256,32]{1,0:T(8,128)S(1)}, f32[32,32]{0,1:T(8,128)S(1)}, f32[32]{0:T(128)S(1)}, f32[256]{0:T(256)S(1)}) all-reduce(f32[256,32]{1,0:T(8,128)S(1)} %fusion.2054, f32[32,32]{0,1:T(8,128)S(1)} %fusion.2055, f32[32]{0:T(128)S(1)} %convolution_bitcast_fusion.2, ...), channel_id=1, replica_groups=mesh['rows'=128,'sub'=4] {'rows','sub'}, use_global_device_ids=true, to_apply=%region_1.0 | all-reduce | flops 9504 | bytes 76032 | tf_op jit(solution)/shard_map/psum | solution.py:68
  122.7 2.9 cholesky.201
  135.2 1.7 fusion.34
  137.3 1.7 fusion.36
  140.3 460.4 %all-reduce.103.cloned.1.call-done = (f32[288,288]{0,1:T(8,128)}, f32[288,288]{0,1:T(8,128)}) async-done(((f32[288,288]{0,1:T(8,128)}, f32[288,288]{0,1:T(8,128)}), (f32[288,288]{0,1:T(8,128)}, f32[288,288]{0,1:T(8,128)})) %all-reduce.103.cloned.1.call-update) | async-done | bytes 663568 | tf_op jit(solution)/shard_map/psum | solution.py:79
  600.7 1.3 copy.58
  603.9 11.7 %cholesky.370 = f32[128,128]{1,0:T(8,128)S(1)} custom-call(f32[128,128]{1,0:T(8,128)S(1)} %cholesky.480), custom_call_target="Cholesky" | custom-call | tf_op jit(solution)/shard_map/jit(cholesky)/cholesky | solution.py:53
  615.7 11.7 %cholesky.427 = f32[128,128]{1,0:T(8,128)S(1)} custom-call(f32[128,128]{1,0:T(8,128)S(1)} %cholesky.488), custom_call_target="Cholesky" | custom-call | tf_op jit(solution)/shard_map/jit(cholesky)/cholesky | solution.py:52
  627.5 10.0 %custom-call.231 = f32[1,128,128]{1,2,0:T(8,128)S(1)} custom-call(f32[1,128,128]{2,1,0:T(8,128)S(1)} %get-tuple-element.119), custom_call_target="InvertDiagBlocksLowerTriangular" | custom-call | tf_op jit(solution)/shard_map/jit(cholesky)/cholesky | solution.py:53
  637.5 1.1 constant_dynamic-update-slice_fusion.3
  638.6 1.2 convolution_subtract_fusion.1
  639.8 11.7 %cholesky.389 = f32[128,128]{1,0:T(8,128)S(1)} custom-call(f32[128,128]{1,0:T(8,128)S(1)} %cholesky.484), custom_call_target="Cholesky" | custom-call | tf_op jit(solution)/shard_map/jit(cholesky)/cholesky | solution.py:53
  651.5 9.8 %custom-call.232 = f32[1,128,128]{1,2,0:T(8,128)S(1)} custom-call(f32[1,128,128]{2,1,0:T(8,128)S(1)} %get-tuple-element.116), custom_call_target="InvertDiagBlocksLowerTriangular" | custom-call | tf_op jit(solution)/shard_map/jit(cholesky)/cholesky | solution.py:53
  662.4 2.9 cholesky.411
  667.3 9.8 %custom-call.233 = f32[1,128,128]{1,2,0:T(8,128)S(1)} custom-call(f32[1,128,128]{2,1,0:T(8,128)S(1)} %get-tuple-element.114), custom_call_target="InvertDiagBlocksLowerTriangular" | custom-call | tf_op jit(solution)/shard_map/jit(cholesky)/cholesky | solution.py:52
  677.6 11.9 %cholesky.446 = f32[128,128]{1,0:T(8,128)S(1)} custom-call(f32[128,128]{1,0:T(8,128)S(1)} %cholesky.492), custom_call_target="Cholesky" | custom-call | tf_op jit(solution)/shard_map/jit(cholesky)/cholesky | solution.py:52
  689.6 9.8 %custom-call.234 = f32[1,128,128]{1,2,0:T(8,128)S(1)} custom-call(f32[1,128,128]{2,1,0:T(8,128)S(1)} %get-tuple-element.111), custom_call_target="InvertDiagBlocksLowerTriangular" | custom-call | tf_op jit(solution)/shard_map/jit(cholesky)/cholesky | solution.py:52
  699.7 2.9 cholesky.468
  711.7 12.1 %cholesky.218 = f32[128,128]{1,0:T(8,128)S(1)} custom-call(f32[128,128]{1,0:T(8,128)S(1)} %cholesky.496), custom_call_target="Cholesky" | custom-call | tf_op jit(solution)/shard_map/jit(cholesky)/cholesky | solution.py:56
  723.8 9.8 %custom-call.28 = f32[1,128,128]{1,2,0:T(8,128)S(1)} custom-call(f32[1,128,128]{2,1,0:T(8,128)S(1)} %get-tuple-element.109), custom_call_target="InvertDiagBlocksLowerTriangular" | custom-call | tf_op jit(solution)/shard_map/jit(cholesky)/cholesky | solution.py:56
  734.1 11.7 %cholesky.284 = f32[128,128]{1,0:T(8,128)S(1)} custom-call(f32[128,128]{1,0:T(8,128)S(1)} %convolution_subtract_fusion.2), custom_call_target="Cholesky" | custom-call | tf_op jit(solution)/shard_map/jit(cholesky)/cholesky | solution.py:56
  937.4 1.3 fusion.35
  948.7 1.3 fusion.33
  (1180 shorter events, 223.9 us)
Async XLA Ops:
  7.2 0.8 copy-start
  7.2 3.3 copy-start.2
  7.2 593.5 %all-reduce.103.cloned.1.call-start = ((), (), s32[]{:S(2)}) async-start(), calls=%async_computation | async-start | bytes 1769472 | tf_op jit(solution)/shard_map/psum | solution.py:79
  9.6 0.7 copy-start.7
  135.2 1.7 copy-start.1
  135.2 1.7 copy-start.6
  600.7 1.3 copy-start.3
  602.0 1.0 copy-start.4
  603.2 0.8 copy-start.5
Sparse Core Ops, SparseCore 0:
  139.2 461.5 all-reduce.102
where the time goes:
time: 967 us; the launch traced here: 957 us
  waiting for transfers between devices  460 us (48%)
  matrix products  151 us (16%)
  other arithmetic  141 us (15%)
  blocking collectives  112 us (12%)
  local copies, waits for them, and re-layouts  71.2 us (7%)
  between operations  21.2 us (2%)
    psum x1, waiting for transfers between devices, on_device(): sent_a, sent_b = lax.psum((sent_a, sent_b), ('rows', 'sub'))  460 us
    dot_general x814, matrix products, matmul(): jnp.dot(left, right, precision=lax.Precision.HIGHEST, preferred_element_t...  147 us
    psum x1, blocking collectives, on_device(): lax.psum((sent_v, proj, proj_r, gram_r), ('rows', 'sub'))  112 us
    gather x100, local copies, waits for them, and re-layouts, small_inverse(): diag_inv = 1.0 / jnp.diagonal(lower)  65.3 us
    another operation x11, other arithmetic, truncate(): low_a = jnp.linalg.cholesky(gram_a)  48.2 us
    another operation x11, other arithmetic, truncate(): low_b = jnp.linalg.cholesky(gram_b)  48.2 us
    another operation x7, other arithmetic, truncate(): low_y = jnp.linalg.cholesky(matmul(start.T, start))  35 us
  transfers between devices with their start and end apart: 1, of which 1 were waited for; matrix products, arithmetic and copies ran while one was open for 0% of the time, Pallas kernels for 0%

commit v1 on v0

--- a/solution.py
+++ b/solution.py
@@ -76,7 +76,7 @@
     gram_b = matmul(wide_b.T, wide_b)
     sent_a = gram_a
     sent_b = gram_b
-    sent_a, sent_b = lax.psum((sent_a, sent_b), ("rows", "sub"))
+    sent_a, sent_b = lax.psum(lax.psum((sent_a, sent_b), "sub"), "rows")
     gram_a = sent_a
     gram_b = sent_b
     coeffs = -matmul(inv_v, gram_r)

time: 967 us -> 899 us (0.930)
  waiting for transfers between devices: 460 us -> 398 us
    psum x1 -> x2, waiting for transfers between devices: 460 us -> 398 us  [on_device(): sent_a, sent_b = lax.psum(lax.psum((sent_a, sent_b), 'sub'), 'rows')]
  transfers between devices with their start and end apart: 1 -> 2, of which waited for: 1 -> 2; matrix products, arithmetic and copies ran while one was open for 0% -> 0% of each run, Pallas kernels for 0% -> 0%
where the time goes in v1:
time: 899 us; the launch traced here: 895 us
  waiting for transfers between devices  398 us (44%)
  matrix products  151 us (17%)
  other arithmetic  141 us (16%)
  blocking collectives  112 us (12%)
  local copies, waits for them, and re-layouts  71 us (8%)
  between operations  21 us (2%)
    psum x2, waiting for transfers between devices, on_device(): sent_a, sent_b = lax.psum(lax.psum((sent_a, sent_b), 'sub'), 'rows')  398 us
    dot_general x814, matrix products, matmul(): jnp.dot(left, right, precision=lax.Precision.HIGHEST, preferred_element_t...  147 us
    psum x1, blocking collectives, on_device(): lax.psum((sent_v, proj, proj_r, gram_r), ('rows', 'sub'))  112 us
    gather x100, local copies, waits for them, and re-layouts, small_inverse(): diag_inv = 1.0 / jnp.diagonal(lower)  65.1 us
    another operation x11, other arithmetic, truncate(): low_a = jnp.linalg.cholesky(gram_a)  48.2 us
    another operation x11, other arithmetic, truncate(): low_b = jnp.linalg.cholesky(gram_b)  48.2 us
    another operation x7, other arithmetic, truncate(): low_y = jnp.linalg.cholesky(matmul(start.T, start))  35 us
  transfers between devices with their start and end apart: 2, of which 2 were waited for; matrix products, arithmetic and copies ran while one was open for 0% of the time, Pallas kernels for 0%

profile of v1, /device:TPU:1, one launch (start us, length us, event | category | flops | bytes accessed | tf_op | source)
XLA Modules:
  0.0 894.7 jit_solution(1189734139356255894)
XLA Ops:
  8.1 1.5 fusion.2054
  10.7 111.9 %all-reduce.99 = (f32[256,32]{1,0:T(8,128)S(1)}, f32[32,32]{0,1:T(8,128)S(1)}, f32[32]{0:T(128)S(1)}, f32[256]{0:T(256)S(1)}) all-reduce(f32[256,32]{1,0:T(8,128)S(1)} %fusion.2054, f32[32,32]{0,1:T(8,128)S(1)} %fusion.2055, f32[32]{0:T(128)S(1)} %convolution_bitcast_fusion.2, ...), channel_id=1, replica_groups=mesh['rows'=128,'sub'=4] {'rows','sub'}, use_global_device_ids=true, to_apply=%region_1.0 | all-reduce | flops 9504 | bytes 76032 | tf_op jit(solution)/shard_map/psum | solution.py:68
  122.7 2.9 cholesky.201
  135.2 1.7 fusion.34
  137.3 1.7 fusion.36
  140.2 50.6 %all-reduce.107.cloned.1.call-done = (f32[288,288]{0,1:T(8,128)}, f32[288,288]{0,1:T(8,128)}) async-done(((f32[288,288]{0,1:T(8,128)}, f32[288,288]{0,1:T(8,128)}), (f32[288,288]{0,1:T(8,128)}, f32[288,288]{0,1:T(8,128)})) %all-reduce.107.cloned.1.call-update) | async-done | bytes 663568 | tf_op jit(solution)/shard_map/psum | solution.py:79
  191.4 347.0 %all-reduce.105.cloned.1.call-done = (f32[288,288]{0,1:T(8,128)}, f32[288,288]{0,1:T(8,128)}) async-done(((f32[288,288]{0,1:T(8,128)}, f32[288,288]{0,1:T(8,128)}), (f32[288,288]{0,1:T(8,128)}, f32[288,288]{0,1:T(8,128)})) %all-reduce.105.cloned.1.call-update) | async-done | bytes 663568 | tf_op jit(solution)/shard_map/psum | solution.py:79
  538.4 1.3 copy.58
  541.6 11.7 %cholesky.370 = f32[128,128]{1,0:T(8,128)S(1)} custom-call(f32[128,128]{1,0:T(8,128)S(1)} %cholesky.480), custom_call_target="Cholesky" | custom-call | tf_op jit(solution)/shard_map/jit(cholesky)/cholesky | solution.py:53
  553.4 11.7 %cholesky.427 = f32[128,128]{1,0:T(8,128)S(1)} custom-call(f32[128,128]{1,0:T(8,128)S(1)} %cholesky.488), custom_call_target="Cholesky" | custom-call | tf_op jit(solution)/shard_map/jit(cholesky)/cholesky | solution.py:52
  565.2 9.8 %custom-call.231 = f32[1,128,128]{1,2,0:T(8,128)S(1)} custom-call(f32[1,128,128]{2,1,0:T(8,128)S(1)} %get-tuple-element.121), custom_call_target="InvertDiagBlocksLowerTriangular" | custom-call | tf_op jit(solution)/shard_map/jit(cholesky)/cholesky | solution.py:53
  576.1 1.2 convolution_subtract_fusion.1
  577.3 11.9 %cholesky.389 = f32[128,128]{1,0:T(8,128)S(1)} custom-call(f32[128,128]{1,0:T(8,128)S(1)} %cholesky.484), custom_call_target="Cholesky" | custom-call | tf_op jit(solution)/shard_map/jit(cholesky)/cholesky | solution.py:53
  589.2 9.8 %custom-call.232 = f32[1,128,128]{1,2,0:T(8,128)S(1)} custom-call(f32[1,128,128]{2,1,0:T(8,128)S(1)} %get-tuple-element.118), custom_call_target="InvertDiagBlocksLowerTriangular" | custom-call | tf_op jit(solution)/shard_map/jit(cholesky)/cholesky | solution.py:53
  600.0 2.9 cholesky.411
  605.0 9.8 %custom-call.233 = f32[1,128,128]{1,2,0:T(8,128)S(1)} custom-call(f32[1,128,128]{2,1,0:T(8,128)S(1)} %get-tuple-element.116), custom_call_target="InvertDiagBlocksLowerTriangular" | custom-call | tf_op jit(solution)/shard_map/jit(cholesky)/cholesky | solution.py:52
  615.3 11.7 %cholesky.446 = f32[128,128]{1,0:T(8,128)S(1)} custom-call(f32[128,128]{1,0:T(8,128)S(1)} %cholesky.492), custom_call_target="Cholesky" | custom-call | tf_op jit(solution)/shard_map/jit(cholesky)/cholesky | solution.py:52
  627.1 10.0 %custom-call.234 = f32[1,128,128]{1,2,0:T(8,128)S(1)} custom-call(f32[1,128,128]{2,1,0:T(8,128)S(1)} %get-tuple-element.113), custom_call_target="InvertDiagBlocksLowerTriangular" | custom-call | tf_op jit(solution)/shard_map/jit(cholesky)/cholesky | solution.py:52
  637.4 2.9 cholesky.468
  649.3 11.7 %cholesky.218 = f32[128,128]{1,0:T(8,128)S(1)} custom-call(f32[128,128]{1,0:T(8,128)S(1)} %cholesky.496), custom_call_target="Cholesky" | custom-call | tf_op jit(solution)/shard_map/jit(cholesky)/cholesky | solution.py:56
  661.1 9.8 %custom-call.28 = f32[1,128,128]{1,2,0:T(8,128)S(1)} custom-call(f32[1,128,128]{2,1,0:T(8,128)S(1)} %get-tuple-element.111), custom_call_target="InvertDiagBlocksLowerTriangular" | custom-call | tf_op jit(solution)/shard_map/jit(cholesky)/cholesky | solution.py:56
  671.4 12.1 %cholesky.284 = f32[128,128]{1,0:T(8,128)S(1)} custom-call(f32[128,128]{1,0:T(8,128)S(1)} %convolution_subtract_fusion.2), custom_call_target="Cholesky" | custom-call | tf_op jit(solution)/shard_map/jit(cholesky)/cholesky | solution.py:56
  875.1 1.3 fusion.35
  886.3 1.3 fusion.33
  (1183 shorter events, 225.4 us)
Async XLA Ops:
  7.2 0.8 copy-start
  7.2 3.3 copy-start.2
  7.2 183.6 %all-reduce.107.cloned.1.call-start = ((), (), s32[]{:S(2)}) async-start(), calls=%async_computation.1 | async-start | bytes 1769472 | tf_op jit(solution)/shard_map/psum | solution.py:79
  9.6 0.7 copy-start.7
  135.2 1.7 copy-start.1
  135.2 1.7 copy-start.6
  139.1 399.4 %all-reduce.105.cloned.1.call-start = ((), (), s32[]{:S(2)}) async-start(), calls=%async_computation | async-start | bytes 1769472 | tf_op jit(solution)/shard_map/psum | solution.py:79
  538.4 1.3 copy-start.3
  539.7 1.0 copy-start.4
  540.8 0.8 copy-start.5
Sparse Core Ops, SparseCore 0:
  139.2 51.5 all-reduce.106
  194.3 344.0 all-reduce.104
